TPU v7x, 32 devices: a whole 2x2x4 slice. The times are simulated.
32 devices in a mesh: ep: 8 (over y, x, core), tp: 4 (over z).
Axes of the slice: x: 2, y: 2, z: 4, core: 2. Of those that a mesh axis runs over, the one named last changes fastest.
Arguments:
- layer_in: bfloat16 [2048, 2048], P('ep', 'tp'), may hold values from -6 to 6
- token_order: int32 [2048], replicated, may hold values from 0 to 2047, as said below
- seq_lengths: int32 [16, 3], P('ep'), may hold values from 1 to 64, 128 in all within a row
- routes: int32 [2048, 8], P('ep'), may hold values from 0 to 15, all different within a row; in each aligned block of 128 rows (0 to 127, 128 to 255, ...) at most 80 rows name the same one
- route_weights: float32 [2048, 8], P('ep'), may hold values from 0.25 to 0.75
- w_query: bfloat16 [2048, 4096], P('ep', 'tp'), may hold values from -0.125 to 0.125
- w_key: bfloat16 [2048, 512], P('ep', 'tp'), may hold values from -0.125 to 0.125
- w_value: bfloat16 [2048, 512], P('ep', 'tp'), may hold values from -0.125 to 0.125
- w_out: bfloat16 [2048, 4096], P('ep', 'tp'), may hold values from -0.5 to 0.5
- norm_attn: bfloat16 [2048], P('ep'), may hold values from 0.5 to 1.5
- norm_moe: bfloat16 [2048], P('ep'), may hold values from 0.5 to 1.5
- query_gain: bfloat16 [128], P('ep'), may hold values from 1 to 1.796875
- key_gain: bfloat16 [128], P('ep'), may hold values from 1 to 1.796875
- w_gate: bfloat16 [16, 768, 2048], P('ep', 'tp'), may hold values from -0.125 to 0.125
- w_up: bfloat16 [16, 768, 2048], P('ep', 'tp'), may hold values from -0.125 to 0.125
- w_down: bfloat16 [16, 768, 2048], P('ep', 'tp'), may hold values from -0.3125 to 0.3125
- grad_out: bfloat16 [2048, 2048], P('ep', 'tp'), may hold values from -6 to 6
Outputs:
- layer_out: bfloat16 [2048, 2048], P('ep', 'tp')
- grad_layer_in: float32 [2048, 2048], P('ep', 'tp')
- grad_w_query: float32 [2048, 4096], P('ep', 'tp')
- grad_w_key: float32 [2048, 512], P('ep', 'tp')
- grad_w_value: float32 [2048, 512], P('ep', 'tp')
- grad_w_out: float32 [2048, 4096], P('ep', 'tp')
- grad_norm_attn: float32 [2048], P('ep')
- grad_norm_moe: float32 [2048], P('ep')
- grad_query_gain: float32 [128], P('ep')
- grad_key_gain: float32 [128], P('ep')
- grad_w_gate: float32 [16, 768, 2048], P('ep', 'tp')
- grad_w_up: float32 [16, 768, 2048], P('ep', 'tp')
- grad_w_down: float32 [16, 768, 2048], P('ep', 'tp')
Inputs may be any that keep to these rules, and one draw needn't show every extreme that they name: `token_order`: each row number appears once. Of the 256 dealt rows of one index of ep, exactly 32 are rows of each index of ep. `seq_lengths`: row b holds the lengths of the 3 sequences of block b of 128 dealt rows, in order; they sum to 128, and the longest is 64. `routes`: each row names 8 different experts. Within each aligned block of 128 dealt rows (one micro-batch of one index of ep) no expert is named by more than 80 rows; in some blocks one is named by exactly 80.
All inputs are finite; a program needn't handle non-finite values.
Results may differ from a plain program's by a relative error of at most 0.023.
Values may be sent and summed in bfloat16 or wider, within the bound.
A program may use at most 256 MiB of HBM per device.

v0:
```python
import jax
import jax.numpy as jnp
from jax import lax
from jax.sharding import PartitionSpec as P

HEAD_DIM = 128
MICRO = 2
F32 = jnp.float32
BF16 = jnp.bfloat16
epsilon = 1e-06
rope_base = 1000000.0


def positions_of(lengths, row_count):
    offsets = jnp.arange(row_count, dtype=jnp.int32)
    seq_ends = jnp.cumsum(lengths)
    segment = jnp.sum((offsets[:, None] >= seq_ends[None, :]).astype(jnp.int32), axis=1)
    starts = seq_ends - lengths
    in_segment = segment[:, None] == jnp.arange(lengths.shape[0], dtype=jnp.int32)[None, :]
    position = offsets - jnp.sum(jnp.where(in_segment, starts[None, :], 0), axis=1)
    return (segment, position)


def rope_tables(position, half_dim):
    frequency = rope_base ** (-jnp.arange(half_dim, dtype=F32) / half_dim)
    angles = position.astype(F32)[:, None] * frequency[None, :]
    return (jnp.cos(angles)[:, None, :], jnp.sin(angles)[:, None, :])


def rotate(values, cosine, sine_table):
    half_dim = values.shape[-1] // 2
    first_half = values[..., :half_dim]
    second_half = values[..., half_dim:]
    return jnp.concatenate(
        [
            first_half * cosine - second_half * sine_table,
            second_half * cosine + first_half * sine_table,
        ],
        axis=-1,
    )


def rotate_back(incoming, cosine, sine_table):
    return rotate(incoming, cosine, -sine_table)


def deal_matrices(token_order, ep_index, rows_dev, ep_count):
    per_pair = rows_dev // ep_count
    rows = jnp.arange(rows_dev, dtype=jnp.int32)
    home = ep_index * rows_dev + rows
    at = jnp.arange(token_order.shape[0], dtype=jnp.int32)
    place = jnp.sum(jnp.where(token_order[None, :] == home[:, None], at[None, :], 0), axis=1)
    dest = place // rows_dev
    rank = jnp.sum(
        ((dest[:, None] == dest[None, :]) & (place[None, :] < place[:, None])).astype(jnp.int32),
        axis=1,
    )
    send_slot = dest * per_pair + rank
    send = (send_slot[None, :] == rows[:, None]).astype(BF16)
    mine = lax.dynamic_slice_in_dim(token_order, ep_index * rows_dev, rows_dev, 0)
    source = mine // rows_dev
    my_rank = jnp.sum(
        ((source[:, None] == source[None, :]) & (rows[None, :] < rows[:, None])).astype(jnp.int32),
        axis=1,
    )
    recv_slot = source * per_pair + my_rank
    recv = (recv_slot[:, None] == rows[None, :]).astype(BF16)
    return (send, recv)


def inverse_rms(values):
    return lax.rsqrt(jnp.mean(values * values, axis=-1, keepdims=True) + epsilon)


def norm_back(grad_unit, unit_values, inverse):
    return inverse * (
        grad_unit - unit_values * jnp.mean(grad_unit * unit_values, axis=-1, keepdims=True)
    )


def dot_nn(left, right):
    return jnp.dot(left, right, preferred_element_type=F32)


def dot_tn(left_rows, right_rows):
    return lax.dot_general(
        left_rows, right_rows, (((0,), (0,)), ((), ())), preferred_element_type=F32
    )


def dot_nt(left_rows, right_matrix):
    return lax.dot_general(
        left_rows, right_matrix, (((1,), (1,)), ((), ())), preferred_element_type=F32
    )


def permute_rows(matrix, rows):
    return dot_nn(matrix, rows).astype(BF16)


def exchange(rows, ep_count):
    split = rows.reshape(ep_count, rows.shape[0] // ep_count, rows.shape[1])
    moved = lax.all_to_all(split, "ep", split_axis=0, concat_axis=0, tiled=True)
    return moved.reshape(rows.shape)


def on_device(
    layer_in,
    token_order,
    seq_lengths,
    routes,
    route_weights,
    w_query,
    w_key,
    w_value,
    w_out,
    norm_attn,
    norm_moe,
    query_gain,
    key_gain,
    w_gate,
    w_up,
    w_down,
    grad_out,
):
    ep_count = lax.axis_size("ep")
    tp_count = lax.axis_size("tp")
    tp_index = lax.axis_index("tp")
    ep_index = lax.axis_index("ep")
    local_experts, hidden_here, model_width = w_gate.shape
    experts = local_experts * ep_count
    rows_dev = layer_in.shape[0]
    micro_rows = rows_dev // MICRO
    share_width = layer_in.shape[1]
    score_scale = HEAD_DIM ** (-0.5)
    send, recv = deal_matrices(token_order, ep_index, rows_dev, ep_count)
    both = jnp.concatenate([layer_in, grad_out], axis=1)
    got = permute_rows(recv, exchange(permute_rows(send, both), ep_count))
    layer_full = lax.all_gather(got[:, :share_width], "tp", axis=1, tiled=True)
    grad_full = lax.all_gather(got[:, share_width:], "tp", axis=1, tiled=True)
    q_width, kv_width = (w_query.shape[1], w_key.shape[1])
    packed = jnp.concatenate([w_query, w_out, w_key, w_value], axis=1)
    packed = lax.all_gather(packed, "ep", axis=0, tiled=True)
    full_query = packed[:, :q_width]
    full_out = packed[:, q_width : 2 * q_width]
    full_kv = packed[:, 2 * q_width :]
    gains = jnp.concatenate([norm_attn, norm_moe, query_gain, key_gain]).reshape(1, -1)
    gains = lax.all_gather(gains, "ep", axis=0, tiled=True).astype(F32)
    part = norm_attn.shape[0]
    head_part = query_gain.shape[0]
    gain_attn = gains[:, :part].reshape(-1)
    gain_moe = gains[:, part : 2 * part].reshape(-1)
    gain_query = gains[:, 2 * part : 2 * part + head_part].reshape(-1)
    gain_key = gains[:, 2 * part + head_part :].reshape(-1)
    expert_ids = jnp.arange(experts, dtype=jnp.int32)
    dense = jnp.sum(
        jnp.where(routes[:, :, None] == expert_ids[None, None, :], route_weights[:, :, None], 0.0),
        axis=1,
    )
    scale_all = lax.all_gather(dense, "ep", axis=0, tiled=True)
    scale = lax.dynamic_slice_in_dim(scale_all, ep_index * local_experts, local_experts, 1)
    all_grad = lax.all_gather(grad_full, "ep", axis=0, tiled=True)
    heads_here = q_width // HEAD_DIM
    kv_here = kv_width // HEAD_DIM
    group_size = heads_here // kv_here
    segment, position = jax.vmap(positions_of, in_axes=(0, None))(seq_lengths, micro_rows)
    cosine, sine_table = rope_tables(position.reshape(-1), HEAD_DIM // 2)
    layer_float = layer_full.astype(F32)
    inverse_one = inverse_rms(layer_float)
    unit_one = layer_float * inverse_one
    normed = (unit_one * gain_attn).astype(BF16)
    query_proj = dot_nn(normed, full_query).reshape(rows_dev, heads_here, HEAD_DIM)
    kv_proj = dot_nn(normed, full_kv)
    key_proj = kv_proj[:, :kv_width].reshape(rows_dev, kv_here, HEAD_DIM)
    value_proj = kv_proj[:, kv_width:].reshape(rows_dev, kv_here, HEAD_DIM)
    inverse_query = inverse_rms(query_proj)
    unit_query = query_proj * inverse_query
    inverse_key = inverse_rms(key_proj)
    unit_key = key_proj * inverse_key
    queries = (
        rotate(unit_query * gain_query, cosine, sine_table)
        .astype(BF16)
        .reshape(MICRO, micro_rows, kv_here, group_size, HEAD_DIM)
    )
    key_rows = (
        rotate(unit_key * gain_key, cosine, sine_table)
        .astype(BF16)
        .reshape(MICRO, micro_rows, kv_here, HEAD_DIM)
    )
    values = value_proj.astype(BF16).reshape(MICRO, micro_rows, kv_here, HEAD_DIM)
    scores = (
        jnp.einsum("mqkgd,mtkd->mkgqt", queries, key_rows, preferred_element_type=F32) * score_scale
    )
    offsets = jnp.arange(micro_rows, dtype=jnp.int32)
    allowed = (segment[:, :, None] == segment[:, None, :]) & (
        offsets[None, None, :] <= offsets[None, :, None]
    )
    scores = jnp.where(allowed[:, None, None], scores, -1e30)
    row_peak = jnp.max(scores, axis=-1, keepdims=True)
    exponent = jnp.exp(scores - row_peak)
    attn_probs = exponent / jnp.sum(exponent, axis=-1, keepdims=True)
    probs_low = attn_probs.astype(BF16)
    context = jnp.einsum("mkgqt,mtkd->mqkgd", probs_low, values, preferred_element_type=F32)
    context_low = context.reshape(rows_dev, heads_here * HEAD_DIM).astype(BF16)
    attn_part = dot_nt(context_low, full_out)
    attn_out = lax.psum(attn_part.astype(BF16), "tp").astype(F32)
    hidden = layer_float + attn_out
    inverse_two = inverse_rms(hidden)
    unit_two = hidden * inverse_two
    moe_in = (unit_two * gain_moe).astype(BF16)
    all_in = lax.all_gather(moe_in, "ep", axis=0, tiled=True)
    flat = local_experts * hidden_here
    gate_matrix = w_gate.reshape(flat, model_width)
    up_matrix = w_up.reshape(flat, model_width)
    down_matrix = w_down.reshape(flat, model_width)
    row_scale = jnp.repeat(scale, hidden_here, axis=1)
    gate_pre = dot_nt(all_in, gate_matrix)
    up_pre = dot_nt(all_in, up_matrix)
    grad_active = dot_nt(all_grad, down_matrix) * row_scale
    sigmoid_gate = jax.nn.sigmoid(gate_pre)
    silu_gate = gate_pre * sigmoid_gate
    active = (silu_gate * up_pre * row_scale).astype(BF16)
    grad_up_pre = (grad_active * silu_gate).astype(BF16)
    grad_gate_pre = (
        grad_active * up_pre * sigmoid_gate * (1.0 + gate_pre * (1.0 - sigmoid_gate))
    ).astype(BF16)
    grad_partial = dot_nn(grad_gate_pre, gate_matrix) + dot_nn(grad_up_pre, up_matrix)
    grad_partial = lax.psum_scatter(
        grad_partial.astype(BF16), "ep", scatter_dimension=0, tiled=True
    )
    grad_share = lax.psum_scatter(grad_partial, "tp", scatter_dimension=1, tiled=True)
    out_partial = dot_nn(active, down_matrix)
    out_partial = lax.psum_scatter(out_partial.astype(BF16), "ep", scatter_dimension=0, tiled=True)
    mixed = lax.psum_scatter(out_partial, "tp", scatter_dimension=1, tiled=True)
    hidden_share = lax.dynamic_slice_in_dim(hidden, tp_index * share_width, share_width, 1)
    layer_dealt = (hidden_share + mixed.astype(F32)).astype(BF16)
    grad_w_down = dot_tn(active, all_grad).reshape(w_down.shape)
    grad_w_gate = dot_tn(grad_gate_pre, all_in).reshape(w_gate.shape)
    grad_w_up = dot_tn(grad_up_pre, all_in).reshape(w_up.shape)
    grad_float = grad_full.astype(F32)
    grad_moe_in = lax.all_gather(grad_share, "tp", axis=1, tiled=True).astype(F32)
    norm_moe_part = jnp.sum(grad_moe_in * unit_two, axis=0)
    grad_hidden = grad_float + norm_back(grad_moe_in * gain_moe, unit_two, inverse_two)
    grad_attn = grad_hidden.astype(BF16)
    grad_w_out = dot_tn(grad_attn, context_low)
    grad_context = (
        dot_nn(grad_attn, full_out)
        .astype(BF16)
        .reshape(MICRO, micro_rows, kv_here, group_size, HEAD_DIM)
    )
    grad_probs = jnp.einsum("mqkgd,mtkd->mkgqt", grad_context, values, preferred_element_type=F32)
    prob_delta = jnp.sum(attn_probs * grad_probs, axis=-1, keepdims=True)
    grad_scores = (attn_probs * (grad_probs - prob_delta)).astype(BF16)
    grad_queries = (
        jnp.einsum("mkgqt,mtkd->mqkgd", grad_scores, key_rows, preferred_element_type=F32).reshape(
            rows_dev, heads_here, HEAD_DIM
        )
        * score_scale
    )
    grad_keys = (
        jnp.einsum("mkgqt,mqkgd->mtkd", grad_scores, queries, preferred_element_type=F32).reshape(
            rows_dev, kv_here, HEAD_DIM
        )
        * score_scale
    )
    grad_values = jnp.einsum(
        "mkgqt,mqkgd->mtkd", probs_low, grad_context, preferred_element_type=F32
    )
    grad_unit_query = rotate_back(grad_queries, cosine, sine_table)
    grad_unit_key = rotate_back(grad_keys, cosine, sine_table)
    query_gain_part = jnp.sum(grad_unit_query * unit_query, axis=(0, 1))
    key_gain_part = jnp.sum(grad_unit_key * unit_key, axis=(0, 1))
    grad_query_proj = (
        norm_back(grad_unit_query * gain_query, unit_query, inverse_query)
        .reshape(rows_dev, heads_here * HEAD_DIM)
        .astype(BF16)
    )
    grad_key_proj = (
        norm_back(grad_unit_key * gain_key, unit_key, inverse_key)
        .reshape(rows_dev, kv_width)
        .astype(BF16)
    )
    grad_value_proj = grad_values.reshape(rows_dev, kv_width).astype(BF16)
    grad_kv_proj = jnp.concatenate([grad_key_proj, grad_value_proj], axis=1)
    normed_part = dot_nt(grad_query_proj, full_query) + dot_nt(grad_kv_proj, full_kv)
    grad_normed = lax.psum_scatter(
        normed_part.astype(BF16), "tp", scatter_dimension=1, tiled=True
    ).astype(F32)
    grad_packed = jnp.concatenate(
        [
            dot_tn(normed, grad_query_proj).astype(BF16),
            grad_w_out.astype(BF16),
            dot_tn(normed, grad_kv_proj).astype(BF16),
        ],
        axis=1,
    )
    grad_packed = lax.psum_scatter(grad_packed, "ep", scatter_dimension=0, tiled=True).astype(F32)
    start = tp_index * share_width
    gain_share = lax.dynamic_slice_in_dim(gain_attn, start, share_width, 0)
    unit_share = lax.dynamic_slice_in_dim(unit_one, start, share_width, 1)
    hidden_grad_share = lax.dynamic_slice_in_dim(grad_hidden, start, share_width, 1)
    scaled = grad_normed * gain_share
    row_mean = lax.psum(jnp.sum(scaled * unit_share, axis=1), "tp") / model_width
    grad_layer = hidden_grad_share + inverse_one * (scaled - unit_share * row_mean[:, None])
    norm_attn_part = lax.dynamic_update_slice_in_dim(
        jnp.zeros((model_width,), F32), jnp.sum(grad_normed * unit_share, axis=0), start, 0
    )
    small = jnp.concatenate(
        [norm_attn_part, norm_moe_part / tp_count, query_gain_part, key_gain_part]
    )
    small = lax.psum(small, ("ep", "tp"))
    grad_norm_attn = lax.dynamic_slice_in_dim(small, ep_index * part, part, 0)
    grad_norm_moe = lax.dynamic_slice_in_dim(small, model_width + ep_index * part, part, 0)
    grad_query_gain = lax.dynamic_slice_in_dim(
        small, 2 * model_width + ep_index * head_part, head_part, 0
    )
    grad_key_gain = lax.dynamic_slice_in_dim(
        small, 2 * model_width + HEAD_DIM + ep_index * head_part, head_part, 0
    )
    back = jnp.concatenate([layer_dealt, grad_layer.astype(BF16)], axis=1)
    home = exchange(dot_tn(recv, back).astype(BF16), ep_count)
    home = dot_tn(send, home)
    return (
        home[:, :share_width].astype(BF16),
        home[:, share_width:],
        grad_packed[:, :q_width],
        grad_packed[:, 2 * q_width : 2 * q_width + kv_width],
        grad_packed[:, 2 * q_width + kv_width :],
        grad_packed[:, q_width : 2 * q_width],
        grad_norm_attn,
        grad_norm_moe,
        grad_query_gain,
        grad_key_gain,
        grad_w_gate,
        grad_w_up,
        grad_w_down,
    )


def solution(mesh):
    return jax.shard_map(
        on_device,
        mesh=mesh,
        in_specs=(
            P("ep", "tp"),
            P(),
            P("ep", None),
            P("ep", None),
            P("ep", None),
            P("ep", "tp"),
            P("ep", "tp"),
            P("ep", "tp"),
            P("ep", "tp"),
            P("ep"),
            P("ep"),
            P("ep"),
            P("ep"),
            P("ep", "tp", None),
            P("ep", "tp", None),
            P("ep", "tp", None),
            P("ep", "tp"),
        ),
        out_specs=(
            P("ep", "tp"),
            P("ep", "tp"),
            P("ep", "tp"),
            P("ep", "tp"),
            P("ep", "tp"),
            P("ep", "tp"),
            P("ep"),
            P("ep"),
            P("ep"),
            P("ep"),
            P("ep", "tp", None),
            P("ep", "tp", None),
            P("ep", "tp", None),
        ),
        check_vma=False,
    )
```

profile of v0, /device:TPU:0, one launch (start us, length us, event | category | flops | bytes accessed | tf_op | source)
XLA Modules:
  0.0 725.2 jit_solution(13505523342195663563)
XLA Ops:
  11.5 5.2 all-to-all-start
  18.4 7.9 %all-to-all-done = bf16[8,32,1024]{2,1,0:T(8,128)(2,1)S(1)} async-done(((bf16[8,32,1024]{2,1,0:T(8,128)(2,1)}), bf16[8,32,1024]{2,1,0:T(8,128)(2,1)S(1)}, u32[]{:S(2)}, u32[]{:S(2)}) %all-to-all-start) | async-done | bytes 524320 | tf_op jit(solution)/shard_map/all_to_all | solution.py:103
  30.8 23.5 %all-reduce = bf16[4352]{0:T(1024)(128)(2,1)S(1)} all-reduce(bf16[4352]{0:T(1024)(128)(2,1)S(1)} %dynamic-update-slice), channel_id=2, replica_groups=mesh['ep'=8,'tp'=4] {'ep'}, use_global_device_ids=true, to_apply=%add | all-reduce | flops 4352 | bytes 17408
  59.1 56.6 %all-gather.10.cloned.1.call-done = bf16[2048,2304]{1,0:T(8,128)(2,1)} async-done(((bf16[256,2304]{1,0:T(8,128)(2,1)}), bf16[2048,2304]{1,0:T(8,128)(2,1)}) %all-gather.10.cloned.1.call-update) | async-done | bytes 9437200 | tf_op jit(solution)/shard_map/all_gather | solution.py:143
  135.1 4.6 fusion.10
  139.8 6.0 all-gather.14.cloned.1.call-done
  147.2 52.7 %all-reduce.3.cloned.1.call-done = bf16[256,2048]{1,0:T(8,128)(2,1)} async-done(((bf16[256,2048]{1,0:T(8,128)(2,1)}), bf16[256,2048]{1,0:T(8,128)(2,1)}) %all-reduce.3.cloned.1.call-update) | async-done | bytes 1048592 | tf_op jit(solution)/shard_map/psum | solution.py:206
  200.0 3.8 convert_add_fusion
  206.7 10.0 %all_gather.28 = f32[2048,16]{0,1:T(8,128)S(1)} all-gather(f32[256,16]{0,1:T(8,128)S(1)} %select_reduce_fusion.1), channel_id=1, replica_groups=mesh['ep'=8,'tp'=4] {'ep'}, dimensions={0}, use_global_device_ids=true | all-gather | bytes 147456 | tf_op jit(solution)/shard_map/all_gather | solution.py:160
  218.8 3.5 copy.81
  222.3 33.1 %all-gather.16.cloned.1.call-done = bf16[2048,2048]{1,0:T(8,128)(2,1)} async-done(((bf16[256,2048]{1,0:T(8,128)(2,1)}), bf16[2048,2048]{1,0:T(8,128)(2,1)}) %all-gather.16.cloned.1.call-update) | async-done | bytes 8388624 | tf_op jit(solution)/shard_map/all_gather | solution.py:162
  255.5 11.0 %convolution_multiply_fusion = f32[2048,384]{1,0:T(8,128)} fusion(f32[2048,384]{1,0:T(8,128)} %copy.81, bf16[2048,2048]{1,0:T(8,128)(2,1)} %all-gather.16.cloned.1.call-done, bf16[384,2048]{1,0:T(8,128)(2,1)} %bitcast.201), kind=kOutput, calls=%fused_computation.21 | convolution fusion | flops 3222011904 | bytes 16252928 | tf_op jit(solution)/shard_map/dot_general | solution.py:92
  266.4 45.1 %all-gather.12.cloned.1.call-done = bf16[2048,2048]{1,0:T(8,128)(2,1)} async-done(((bf16[256,2048]{1,0:T(8,128)(2,1)}), bf16[2048,2048]{1,0:T(8,128)(2,1)}) %all-gather.12.cloned.1.call-update) | async-done | bytes 8388624 | tf_op jit(solution)/shard_map/all_gather | solution.py:211
  311.5 10.2 %fusion.104 = f32[2048,384]{1,0:T(8,128)} fusion(bf16[2048,2048]{1,0:T(8,128)(2,1)} %all-gather.12.cloned.1.call-done, bf16[384,2048]{1,0:T(8,128)(2,1)} %bitcast.184), kind=kOutput, calls=%fused_computation.204 | convolution fusion | flops 3221225472 | bytes 13107200 | tf_op jit(solution)/shard_map/dot_general | solution.py:92
  321.7 8.5 %multiply_convert_fusion.2 = (bf16[2048,384]{1,0:T(8,128)(2,1)}, bf16[2048,384]{1,0:T(8,128)(2,1)S(1)}, bf16[2048,384]{1,0:T(8,128)(2,1)S(1)}) fusion(f32[2048,384]{1,0:T(8,128)S(1)} %copy-done.24, f32[2048,384]{1,0:T(8,128)} %fusion.104, f32[2048,384]{1,0:T(8,128)S(1)} %copy-done.75, bf16[2048,2048]{1,0:T(8,128)(2,1)S(1)} %copy-done.2, ...), kind=kOutput, calls=%fused_computation.15 | convolution fusion | flops 3233808384 | bytes 24117248 | tf_op jit(solution)/shard_map/dot_general | solution.py:92
  330.2 22.1 %fusion.105 = f32[2048,2048]{1,0:T(8,128)} fusion(bf16[2048,384]{1,0:T(8,128)(2,1)S(1)} %get-tuple-element.61, bf16[384,2048]{1,0:T(8,128)(2,1)S(1)} %bitcast.185), kind=kOutput, calls=%fused_computation.205 | convolution fusion | flops 3221225472 | bytes 19922944 | tf_op jit(solution)/shard_map/dot_general | solution.py:82
  352.3 10.2 %add_convert_fusion = bf16[2048,2048]{1,0:T(8,128)(2,1)} fusion(f32[2048,2048]{1,0:T(8,128)} %fusion.105, bf16[2048,384]{1,0:T(8,128)(2,1)S(1)} %get-tuple-element.62, bf16[384,2048]{1,0:T(8,128)(2,1)S(1)} %bitcast.162), kind=kOutput, calls=%fused_computation | convolution fusion | flops 3229614080 | bytes 28311552 | tf_op jit(solution)/shard_map/dot_general | solution.py:82
  362.6 71.6 %reduce-scatter.11.cloned.1.call-done = bf16[256,2048]{1,0:T(8,128)(2,1)} async-done(((bf16[2048,2048]{1,0:T(8,128)(2,1)}), bf16[256,2048]{1,0:T(8,128)(2,1)}) %reduce-scatter.11.cloned.1.call-update) | async-done | bytes 1048592 | tf_op jit(solution)/shard_map/reduce_scatter | solution.py:228
  434.3 8.1 %convolution_convert_fusion = bf16[2048,2048]{1,0:T(8,128)(2,1)} fusion(bf16[2048,384]{1,0:T(8,128)(2,1)S(1)} %copy-done.25, bf16[384,2048]{1,0:T(8,128)(2,1)} %bitcast.202), kind=kOutput, calls=%fused_computation.2 | convolution fusion | flops 3225419776 | bytes 11534336 | tf_op jit(solution)/shard_map/dot_general | solution.py:82
  442.5 21.3 %reduce-scatter.13.cloned.1.call-done = bf16[256,512]{1,0:T(8,128)(2,1)} async-done(((bf16[256,2048]{1,0:T(8,128)(2,1)}), bf16[256,512]{1,0:T(8,128)(2,1)}) %reduce-scatter.13.cloned.1.call-update) | async-done | bytes 262160 | tf_op jit(solution)/shard_map/reduce_scatter | solution.py:231
  466.2 71.1 %reduce-scatter.7.cloned.1.call-done = bf16[256,2048]{1,0:T(8,128)(2,1)} async-done(((bf16[2048,2048]{1,0:T(8,128)(2,1)}), bf16[256,2048]{1,0:T(8,128)(2,1)}) %reduce-scatter.7.cloned.1.call-update) | async-done | bytes 1048592 | tf_op jit(solution)/shard_map/reduce_scatter | solution.py:233
  537.4 29.4 %all-gather.18.cloned.1.call-done = bf16[256,2048]{1,0:T(8,128)(2,1)} async-done(((bf16[256,512]{1,0:T(8,128)(2,1)}), bf16[256,2048]{1,0:T(8,128)(2,1)}) %all-gather.18.cloned.1.call-update) | async-done | bytes 1048592 | tf_op jit(solution)/shard_map/all_gather | solution.py:241
  570.7 4.3 fusion.26
  584.5 3.5 fusion.4
  594.3 15.9 %pad_maximum_fusion = bf16[2048,2304]{0,1:T(8,128)(2,1)} fusion(bf16[2048,256]{0,1:T(8,128)(2,1)S(1)} %convolution_convert_fusion.3, bf16[2048,1024]{0,1:T(8,128)(2,1)S(1)} %convolution_convert_fusion.1, bf16[2048,1024]{0,1:T(8,128)(2,1)S(1)} %convolution_convert_fusion.2), kind=kLoop, calls=%fused_computation.1 | loop fusion | flops 28311552 | bytes 18874368 | tf_op jit(solution)/shard_map/concatenate | solution.py:289
  611.7 8.7 %fusion.108 = f32[384,2048]{1,0:T(8,128)} fusion(bf16[2048,384]{1,0:T(8,128)(2,1)S(1)} %copy-done.26, bf16[2048,2048]{1,0:T(8,128)(2,1)} %all-gather.16.cloned.1.call-done), kind=kOutput, calls=%fused_computation.208 | convolution fusion | flops 3221225472 | bytes 13107200 | tf_op jit(solution)/shard_map/dot_general | solution.py:86
  620.4 8.8 %fusion.106 = f32[384,2048]{1,0:T(8,128)} fusion(bf16[2048,384]{1,0:T(8,128)(2,1)S(1)} %copy-done.15, bf16[2048,2048]{1,0:T(8,128)(2,1)} %all-gather.12.cloned.1.call-done), kind=kOutput, calls=%fused_computation.206 | convolution fusion | flops 3221225472 | bytes 13107200 | tf_op jit(solution)/shard_map/dot_general | solution.py:86
  629.2 5.3 fusion.107
  637.4 10.4 %psum.22 = f32[256]{0:T(256)S(1)} all-reduce(f32[256]{0:T(256)S(1)} %get-tuple-element.55), channel_id=1, replica_groups=mesh['ep'=8,'tp'=4] {'tp'}, use_global_device_ids=true, to_apply=%region_24.25 | all-reduce | flops 256 | bytes 2048 | tf_op jit(solution)/shard_map/psum | solution.py:303
  650.5 3.6 all-to-all-start.1
  654.4 47.9 %psum.23 = f32[4352]{0:T(1024)S(1)} all-reduce(f32[4352]{0:T(1024)S(1)} %pad_maximum_fusion.10), channel_id=1, replica_groups=mesh['ep'=8,'tp'=4] {'ep','tp'}, use_global_device_ids=true, to_apply=%region_31.32 | all-reduce | flops 4352 | bytes 34816 | tf_op jit(solution)/shard_map/psum | solution.py:311
  705.5 4.1 reduce-scatter.17.cloned.1.call-done
  (303 shorter events, 81.1 us)
Async XLA Ops:
  7.2 314.5 %copy-start = (bf16[2,192,2048]{2,1,0:T(8,128)(2,1)S(1)}, bf16[2,192,2048]{2,1,0:T(8,128)(2,1)}, u32[]{:S(2)}) copy-start(bf16[2,192,2048]{2,1,0:T(8,128)(2,1)} %param.31) | copy-start | bytes 4718596
  9.2 18.5 %copy-start.48 = (bf16[256,128]{1,0:T(8,128)(2,1)S(1)}, bf16[256,128]{1,0:T(8,128)(2,1)}, u32[]{:S(2)}) copy-start(bf16[256,128]{1,0:T(8,128)(2,1)} %param.23) | copy-start | bytes 196612
  11.5 14.9 %all-to-all-start = ((bf16[8,32,1024]{2,1,0:T(8,128)(2,1)}), bf16[8,32,1024]{2,1,0:T(8,128)(2,1)S(1)}, u32[]{:S(2)}, u32[]{:S(2)}) async-start(bf16[8,32,1024]{2,1,0:T(8,128)(2,1)} %bitcast), calls=%async_computation | async-start | bytes 1048576 | tf_op jit(solution)/shard_map/all_to_all | solution.py:103
  16.7 40.8 %all-gather.8.cloned.1.call-start = ((), (), s32[]{:S(2)}) async-start(), calls=%async_computation.8 | async-start | bytes 1310720 | tf_op jit(solution)/shard_map/all_gather | solution.py:139
  27.6 88.1 %all-gather.10.cloned.1.call-start = ((), (), s32[]{:S(2)}) async-start(), calls=%async_computation.9 | async-start | bytes 10616832 | tf_op jit(solution)/shard_map/all_gather | solution.py:143
  28.8 117.0 %all-gather.14.cloned.1.call-start = ((), (), s32[]{:S(2)}) async-start(), calls=%async_computation.14 | async-start | bytes 1310720 | tf_op jit(solution)/shard_map/all_gather | solution.py:140
  54.6 67.5 %copy-start.59 = (f32[128]{0:T(128)}, f32[128]{0:T(128)S(1)}, u32[]{:S(2)}) copy-start(f32[128]{0:T(128)S(1)} %mul.459) | copy-start | bytes 1540
  54.6 67.6 %copy-start.61 = (f32[128]{0:T(128)}, f32[128]{0:T(128)S(1)}, u32[]{:S(2)}) copy-start(f32[128]{0:T(128)S(1)} %mul.473) | copy-start | bytes 1540
  55.3 68.8 %copy-start.63 = (f32[64]{0:T(128)}, f32[64]{0:T(128)S(1)}, u32[]{:S(2)}) copy-start(f32[64]{0:T(128)S(1)} %multiply_power_fusion) | copy-start | bytes 772
  55.5 68.6 %copy-start.52 = (f32[256]{0:T(256)}, f32[256]{0:T(256)S(1)}, u32[]{:S(2)}) copy-start(f32[256]{0:T(256)S(1)} %convert_bitcast_fusion.1) | copy-start | bytes 3076
  57.4 69.3 %copy-start.31 = (f32[256,64]{1,0:T(8,128)}, f32[256,64]{1,0:T(8,128)S(1)}, u32[]{:S(2)}) copy-start(f32[256,64]{1,0:T(8,128)S(1)} %get-tuple-element.94) | copy-start | bytes 196612
  57.4 142.5 %all-reduce.3.cloned.1.call-start = ((), (), s32[]{:S(2)}) async-start(), calls=%async_computation.10 | async-start | bytes 2097152 | tf_op jit(solution)/shard_map/psum | solution.py:206
  57.5 60.5 %copy-start.3 = (bf16[256,2048]{1,0:T(8,128)(2,1)S(1)}, bf16[256,2048]{1,0:T(8,128)(2,1)}, u32[]{:S(2)}) copy-start(bf16[256,2048]{1,0:T(8,128)(2,1)} %all-gather.8.cloned.1.call-done) | copy-start | bytes 3145732
  59.1 62.4 %copy-start.50 = (f32[256]{0:T(256)}, f32[256]{0:T(256)S(1)}, u32[]{:S(2)}) copy-start(f32[256]{0:T(256)S(1)} %add_rsqrt_fusion.3) | copy-start | bytes 3076
  139.8 115.7 %all-gather.16.cloned.1.call-start = ((), (), s32[]{:S(2)}) async-start(), calls=%async_computation.15 | async-start | bytes 9437184 | tf_op jit(solution)/shard_map/all_gather | solution.py:162
  145.9 165.6 %all-gather.12.cloned.1.call-start = ((), (), s32[]{:S(2)}) async-start(), calls=%async_computation.11 | async-start | bytes 9437184 | tf_op jit(solution)/shard_map/all_gather | solution.py:211
  205.9 228.3 %reduce-scatter.11.cloned.1.call-start = ((), (), s32[]{:S(2)}) async-start(), calls=%async_computation.16 | async-start | bytes 9437184 | tf_op jit(solution)/shard_map/reduce_scatter | solution.py:228
  330.2 22.1 %copy-start.14 = (bf16[2048,384]{1,0:T(8,128)(2,1)}, bf16[2048,384]{1,0:T(8,128)(2,1)S(1)}, u32[]{:S(2)}) copy-start(bf16[2048,384]{1,0:T(8,128)(2,1)S(1)} %get-tuple-element.61) | copy-start | bytes 4718596
  330.2 22.1 %copy-start.12 = (bf16[2048,384]{1,0:T(8,128)(2,1)}, bf16[2048,384]{1,0:T(8,128)(2,1)S(1)}, u32[]{:S(2)}) copy-start(bf16[2048,384]{1,0:T(8,128)(2,1)S(1)} %get-tuple-element.62) | copy-start | bytes 4718596
  362.5 71.7 %copy-start.25 = (bf16[2048,384]{1,0:T(8,128)(2,1)S(1)}, bf16[2048,384]{1,0:T(8,128)(2,1)}, u32[]{:S(2)}) copy-start(bf16[2048,384]{1,0:T(8,128)(2,1)} %get-tuple-element.60) | copy-start | bytes 4718596
  362.5 101.3 %reduce-scatter.13.cloned.1.call-start = ((), (), s32[]{:S(2)}) async-start(), calls=%async_computation.17 | async-start | bytes 1310720 | tf_op jit(solution)/shard_map/reduce_scatter | solution.py:231
  434.2 103.1 %reduce-scatter.7.cloned.1.call-start = ((), (), s32[]{:S(2)}) async-start(), calls=%async_computation.12 | async-start | bytes 9437184 | tf_op jit(solution)/shard_map/reduce_scatter | solution.py:233
  442.4 22.7 %copy-start.19 = (bf16[2,8,128,128]{2,3,1,0:T(8,128)(2,1)S(1)}, bf16[2,8,128,128]{2,3,1,0:T(8,128)(2,1)}, u32[]{:S(2)}) copy-start(bf16[2,8,128,128]{2,3,1,0:T(8,128)(2,1)} %copy-done.18) | copy-start | bytes 1572868
  442.4 124.3 %copy-start.11 = (bf16[256,2048]{1,0:T(8,128)(2,1)S(1)}, bf16[256,2048]{1,0:T(8,128)(2,1)}, u32[]{:S(2)}) copy-start(bf16[256,2048]{1,0:T(8,128)(2,1)} %all-reduce.3.cloned.1.call-done) | copy-start | bytes 3145732
  442.4 124.3 %all-gather.18.cloned.1.call-start = ((), (), s32[]{:S(2)}) async-start(), calls=%async_computation.18 | async-start | bytes 1310720 | tf_op jit(solution)/shard_map/all_gather | solution.py:241
  463.8 170.6 %reduce-scatter.9.cloned.1.call-start = ((), (), s32[]{:S(2)}) async-start(), calls=%async_computation.13 | async-start | bytes 1310720 | tf_op jit(solution)/shard_map/reduce_scatter | solution.py:234
  537.3 32.4 %copy-start.43 = (f32[1,2,8,128]{3,1,2,0:T(2,128)S(1)}, f32[1,2,8,128]{3,1,2,0:T(2,128)}, u32[]{:S(2)}) copy-start(f32[1,2,8,128]{3,1,2,0:T(2,128)} %copy.118) | copy-start | bytes 24580
  537.3 32.4 %copy-start.57 = (f32[256]{0:T(256)S(1)}, f32[256]{0:T(256)}, u32[]{:S(2)}) copy-start(f32[256]{0:T(256)} %copy-done.56) | copy-start | bytes 3076
  537.3 98.5 %reduce-scatter.15.cloned.1.call-start = ((), (), s32[]{:S(2)}) async-start(), calls=%async_computation.19 | async-start | bytes 1310720 | tf_op jit(solution)/shard_map/reduce_scatter | solution.py:286
  590.7 118.8 %reduce-scatter.17.cloned.1.call-start = ((), (), s32[]{:S(2)}) async-start(), calls=%async_computation.20 | async-start | bytes 10616832 | tf_op jit(solution)/shard_map/reduce_scatter | solution.py:297
  637.4 66.1 %copy-start.69 = (s32[256]{0:T(256)S(1)}, s32[256]{0:T(256)}, u32[]{:S(2)}) copy-start(s32[256]{0:T(256)} %copy-done.68) | copy-start | bytes 3076
  650.5 53.1 %all-to-all-start.1 = ((bf16[8,32,1024]{2,1,0:T(8,128)(2,1)}), bf16[8,32,1024]{2,1,0:T(8,128)(2,1)S(1)}, u32[]{:S(2)}, u32[]{:S(2)}) async-start(bf16[8,32,1024]{2,1,0:T(8,128)(2,1)} %bitcast.45), calls=%async_computation.6 | async-start | bytes 1048576 | tf_op jit(solution)/shard_map/all_to_all | solution.py:103
  (61 other events, 283.2 us)
Sparse Core Ops, SparseCore 0:
  27.7 27.3 all-gather.7
  57.6 58.0 all-gather.9
  117.9 27.9 all-gather.13
  148.7 51.2 all-reduce.2
  201.7 53.7 all-gather.15
  257.2 54.2 all-gather.11
  362.7 71.4 reduce-scatter.10
  436.5 27.2 reduce-scatter.12
  467.3 69.9 reduce-scatter.6
  538.7 27.9 all-gather.17
  569.0 26.6 reduce-scatter.8
  598.5 25.7 reduce-scatter.14
  627.8 81.7 reduce-scatter.16
where the time goes:
time: 734 us; the launch traced here: 725 us
  waiting for transfers between devices  399 us (54%)
  matrix products  125 us (17%)
  blocking collectives  91.8 us (13%)
  other arithmetic  46.4 us (6%)
  local copies, waits for them, and re-layouts  37.7 us (5%)
  between operations  16.1 us (2%)
  starting transfers between devices  9.33 us (1%)
    reduce_scatter x1, waiting for transfers between devices, on_device(): lax.psum_scatter(grad_partial.astype(BF16), 'ep', scatter_dimension=0, ti...  71.6 us
    reduce_scatter x1, waiting for transfers between devices, on_device(): lax.psum_scatter(out_partial.astype(BF16), 'ep', scatter_dimension=0, til...  71.1 us
    all_gather x1, waiting for transfers between devices, on_device(): packed = lax.all_gather(packed, 'ep', axis=0, tiled=True)  56.6 us
    dot_general x8, matrix products, dot_nn(): return jnp.dot(left, right, preferred_element_type=F32)  52.9 us
    psum x1, waiting for transfers between devices, on_device(): attn_out = lax.psum(attn_part.astype(BF16), 'tp').astype(F32)  52.7 us
    psum x1, blocking collectives, on_device(): small = lax.psum(small, ('ep', 'tp'))  47.9 us
    all_gather x1, waiting for transfers between devices, on_device(): all_in = lax.all_gather(moe_in, 'ep', axis=0, tiled=True)  45.1 us
    dot_general x6, matrix products, dot_nt(): lax.dot_general(left_rows, right_matrix, (((1,), (1,)), ((), ())), prefer...  40.5 us
  transfers between devices with their start and end apart: 15, of which 11 were waited for; matrix products, arithmetic and copies ran while one was open for 19% of the time, Pallas kernels for 0%

commit v1 on v0

--- a/solution.py
+++ b/solution.py
@@ -203,7 +203,7 @@
     context = jnp.einsum("mkgqt,mtkd->mqkgd", probs_low, values, preferred_element_type=F32)
     context_low = context.reshape(rows_dev, heads_here * HEAD_DIM).astype(BF16)
     attn_part = dot_nt(context_low, full_out)
-    attn_out = lax.psum(attn_part.astype(BF16), "tp").astype(F32)
+    attn_out = jnp.sum(lax.all_gather(attn_part.astype(BF16), "tp"), axis=0).astype(F32)
     hidden = layer_float + attn_out
     inverse_two = inverse_rms(hidden)
     unit_two = hidden * inverse_two

time: 734 us -> 761 us (1.037)
  waiting for transfers between devices: 399 us -> 421 us
    all_gather x0 -> x1, waiting for transfers between devices: none -> 80.5 us  [on_device(): lax.all_gather(attn_part.astype(BF16), 'tp')]
    psum x1 -> x0, waiting for transfers between devices: 52.7 us -> none  [on_device(): attn_out = lax.psum(attn_part.astype(BF16), 'tp').astype(F32)]
    unnamed x170 -> x168, local copies, waits for them, and re-layouts: 16.1 us -> 15.5 us
where the time goes in v1:
time: 761 us; the launch traced here: 752 us
  waiting for transfers between devices  421 us (55%)
  matrix products  125 us (16%)
  blocking collectives  91.5 us (12%)
  other arithmetic  51.8 us (7%)
  local copies, waits for them, and re-layouts  37.1 us (5%)
  between operations  16.1 us (2%)
  starting transfers between devices  9.62 us (1%)
    all_gather x1, waiting for transfers between devices, on_device(): lax.all_gather(attn_part.astype(BF16), 'tp')  80.5 us
    reduce_scatter x1, waiting for transfers between devices, on_device(): lax.psum_scatter(grad_partial.astype(BF16), 'ep', scatter_dimension=0, ti...  71.6 us
    reduce_scatter x1, waiting for transfers between devices, on_device(): lax.psum_scatter(out_partial.astype(BF16), 'ep', scatter_dimension=0, til...  71.1 us
    all_gather x1, waiting for transfers between devices, on_device(): packed = lax.all_gather(packed, 'ep', axis=0, tiled=True)  55.5 us
    dot_general x8, matrix products, dot_nn(): return jnp.dot(left, right, preferred_element_type=F32)  52.9 us
    psum x1, blocking collectives, on_device(): small = lax.psum(small, ('ep', 'tp'))  47.9 us
    all_gather x1, waiting for transfers between devices, on_device(): all_in = lax.all_gather(moe_in, 'ep', axis=0, tiled=True)  45.1 us
    dot_general x6, matrix products, dot_nt(): lax.dot_general(left_rows, right_matrix, (((1,), (1,)), ((), ())), prefer...  40.6 us
  transfers between devices with their start and end apart: 15, of which 11 were waited for; matrix products, arithmetic and copies ran while one was open for 19% of the time, Pallas kernels for 0%

profile of v1, /device:TPU:0, one launch (start us, length us, event | category | flops | bytes accessed | tf_op | source)
XLA Modules:
  0.0 752.2 jit_solution(16061345660151406969)
XLA Ops:
  10.9 5.2 all-to-all-start
  17.9 7.9 %all-to-all-done = bf16[8,32,1024]{2,1,0:T(8,128)(2,1)S(1)} async-done(((bf16[8,32,1024]{2,1,0:T(8,128)(2,1)}), bf16[8,32,1024]{2,1,0:T(8,128)(2,1)S(1)}, u32[]{:S(2)}, u32[]{:S(2)}) %all-to-all-start) | async-done | bytes 524320 | tf_op jit(solution)/shard_map/all_to_all | solution.py:103
  31.3 23.5 %all-reduce = bf16[4352]{0:T(1024)(128)(2,1)S(1)} all-reduce(bf16[4352]{0:T(1024)(128)(2,1)S(1)} %dynamic-update-slice), channel_id=2, replica_groups=mesh['ep'=8,'tp'=4] {'ep'}, use_global_device_ids=true, to_apply=%add | all-reduce | flops 4352 | bytes 17408
  59.6 55.5 %all-gather.12.cloned.1.call-done = bf16[2048,2304]{1,0:T(8,128)(2,1)} async-done(((bf16[256,2304]{1,0:T(8,128)(2,1)}), bf16[2048,2304]{1,0:T(8,128)(2,1)}) %all-gather.12.cloned.1.call-update) | async-done | bytes 9437200 | tf_op jit(solution)/shard_map/all_gather | solution.py:143
  117.4 3.6 fusion.6
  134.6 4.6 fusion.10
  139.3 6.0 all-gather.16.cloned.1.call-done
  146.9 80.5 %all-gather.22.cloned.1.call-done = bf16[1024,2048]{1,0:T(8,128)(2,1)} async-done(((bf16[256,2048]{1,0:T(8,128)(2,1)}), bf16[1024,2048]{1,0:T(8,128)(2,1)}) %all-gather.22.cloned.1.call-update) | async-done | bytes 4194320 | tf_op jit(solution)/shard_map/all_gather | solution.py:206
  227.4 4.3 reduce_sum.208
  231.8 3.9 convert_add_fusion
  238.6 9.8 %all_gather.36 = f32[2048,16]{0,1:T(8,128)S(1)} all-gather(f32[256,16]{0,1:T(8,128)S(1)} %select_reduce_fusion.1), channel_id=1, replica_groups=mesh['ep'=8,'tp'=4] {'ep'}, dimensions={0}, use_global_device_ids=true | all-gather | bytes 147456 | tf_op jit(solution)/shard_map/all_gather | solution.py:160
  254.0 28.5 %all-gather.18.cloned.1.call-done = bf16[2048,2048]{1,0:T(8,128)(2,1)} async-done(((bf16[256,2048]{1,0:T(8,128)(2,1)}), bf16[2048,2048]{1,0:T(8,128)(2,1)}) %all-gather.18.cloned.1.call-update) | async-done | bytes 8388624 | tf_op jit(solution)/shard_map/all_gather | solution.py:162
  282.5 11.0 %convolution_multiply_fusion = f32[2048,384]{1,0:T(8,128)} fusion(f32[2048,384]{1,0:T(8,128)} %copy.81, bf16[2048,2048]{1,0:T(8,128)(2,1)} %all-gather.18.cloned.1.call-done, bf16[384,2048]{1,0:T(8,128)(2,1)} %bitcast.203), kind=kOutput, calls=%fused_computation.21 | convolution fusion | flops 3222011904 | bytes 16252928 | tf_op jit(solution)/shard_map/dot_general | solution.py:92
  293.5 45.1 %all-gather.14.cloned.1.call-done = bf16[2048,2048]{1,0:T(8,128)(2,1)} async-done(((bf16[256,2048]{1,0:T(8,128)(2,1)}), bf16[2048,2048]{1,0:T(8,128)(2,1)}) %all-gather.14.cloned.1.call-update) | async-done | bytes 8388624 | tf_op jit(solution)/shard_map/all_gather | solution.py:211
  338.5 10.2 %fusion.104 = f32[2048,384]{1,0:T(8,128)} fusion(bf16[2048,2048]{1,0:T(8,128)(2,1)} %all-gather.14.cloned.1.call-done, bf16[384,2048]{1,0:T(8,128)(2,1)} %bitcast.186), kind=kOutput, calls=%fused_computation.204 | convolution fusion | flops 3221225472 | bytes 13107200 | tf_op jit(solution)/shard_map/dot_general | solution.py:92
  348.7 8.5 %multiply_convert_fusion.2 = (bf16[2048,384]{1,0:T(8,128)(2,1)}, bf16[2048,384]{1,0:T(8,128)(2,1)S(1)}, bf16[2048,384]{1,0:T(8,128)(2,1)S(1)}) fusion(f32[2048,384]{1,0:T(8,128)S(1)} %copy-done.24, f32[2048,384]{1,0:T(8,128)} %fusion.104, f32[2048,384]{1,0:T(8,128)S(1)} %copy-done.74, bf16[2048,2048]{1,0:T(8,128)(2,1)S(1)} %copy-done.2, ...), kind=kOutput, calls=%fused_computation.15 | convolution fusion | flops 3233808384 | bytes 24117248 | tf_op jit(solution)/shard_map/dot_general | solution.py:92
  357.3 22.0 %fusion.105 = f32[2048,2048]{1,0:T(8,128)} fusion(bf16[2048,384]{1,0:T(8,128)(2,1)S(1)} %get-tuple-element.61, bf16[384,2048]{1,0:T(8,128)(2,1)S(1)} %bitcast.187), kind=kOutput, calls=%fused_computation.205 | convolution fusion | flops 3221225472 | bytes 19922944 | tf_op jit(solution)/shard_map/dot_general | solution.py:82
  379.2 10.2 %add_convert_fusion = bf16[2048,2048]{1,0:T(8,128)(2,1)} fusion(f32[2048,2048]{1,0:T(8,128)} %fusion.105, bf16[2048,384]{1,0:T(8,128)(2,1)S(1)} %get-tuple-element.62, bf16[384,2048]{1,0:T(8,128)(2,1)S(1)} %bitcast.163), kind=kOutput, calls=%fused_computation | convolution fusion | flops 3229614080 | bytes 28311552 | tf_op jit(solution)/shard_map/dot_general | solution.py:82
  389.5 71.6 %reduce-scatter.11.cloned.1.call-done = bf16[256,2048]{1,0:T(8,128)(2,1)} async-done(((bf16[2048,2048]{1,0:T(8,128)(2,1)}), bf16[256,2048]{1,0:T(8,128)(2,1)}) %reduce-scatter.11.cloned.1.call-update) | async-done | bytes 1048592 | tf_op jit(solution)/shard_map/reduce_scatter | solution.py:228
  461.2 8.1 %convolution_convert_fusion = bf16[2048,2048]{1,0:T(8,128)(2,1)} fusion(bf16[2048,384]{1,0:T(8,128)(2,1)S(1)} %copy-done.25, bf16[384,2048]{1,0:T(8,128)(2,1)} %bitcast.204), kind=kOutput, calls=%fused_computation.2 | convolution fusion | flops 3225419776 | bytes 11534336 | tf_op jit(solution)/shard_map/dot_general | solution.py:82
  469.4 21.3 %reduce-scatter.13.cloned.1.call-done = bf16[256,512]{1,0:T(8,128)(2,1)} async-done(((bf16[256,2048]{1,0:T(8,128)(2,1)}), bf16[256,512]{1,0:T(8,128)(2,1)}) %reduce-scatter.13.cloned.1.call-update) | async-done | bytes 262160 | tf_op jit(solution)/shard_map/reduce_scatter | solution.py:231
  493.1 71.1 %reduce-scatter.7.cloned.1.call-done = bf16[256,2048]{1,0:T(8,128)(2,1)} async-done(((bf16[2048,2048]{1,0:T(8,128)(2,1)}), bf16[256,2048]{1,0:T(8,128)(2,1)}) %reduce-scatter.7.cloned.1.call-update) | async-done | bytes 1048592 | tf_op jit(solution)/shard_map/reduce_scatter | solution.py:233
  564.3 29.4 %all-gather.20.cloned.1.call-done = bf16[256,2048]{1,0:T(8,128)(2,1)} async-done(((bf16[256,512]{1,0:T(8,128)(2,1)}), bf16[256,2048]{1,0:T(8,128)(2,1)}) %all-gather.20.cloned.1.call-update) | async-done | bytes 1048592 | tf_op jit(solution)/shard_map/all_gather | solution.py:241
  597.6 4.3 fusion.26
  621.3 15.9 %pad_maximum_fusion = bf16[2048,2304]{0,1:T(8,128)(2,1)} fusion(bf16[2048,256]{0,1:T(8,128)(2,1)S(1)} %convolution_convert_fusion.3, bf16[2048,1024]{0,1:T(8,128)(2,1)S(1)} %convolution_convert_fusion.1, bf16[2048,1024]{0,1:T(8,128)(2,1)S(1)} %convolution_convert_fusion.2), kind=kLoop, calls=%fused_computation.1 | loop fusion | flops 28311552 | bytes 18874368 | tf_op jit(solution)/shard_map/concatenate | solution.py:289
  638.6 8.7 %fusion.108 = f32[384,2048]{1,0:T(8,128)} fusion(bf16[2048,384]{1,0:T(8,128)(2,1)S(1)} %copy-done.26, bf16[2048,2048]{1,0:T(8,128)(2,1)} %all-gather.18.cloned.1.call-done), kind=kOutput, calls=%fused_computation.208 | convolution fusion | flops 3221225472 | bytes 13107200 | tf_op jit(solution)/shard_map/dot_general | solution.py:86
  647.3 8.8 %fusion.106 = f32[384,2048]{1,0:T(8,128)} fusion(bf16[2048,384]{1,0:T(8,128)(2,1)S(1)} %copy-done.15, bf16[2048,2048]{1,0:T(8,128)(2,1)} %all-gather.14.cloned.1.call-done), kind=kOutput, calls=%fused_computation.206 | convolution fusion | flops 3221225472 | bytes 13107200 | tf_op jit(solution)/shard_map/dot_general | solution.py:86
  656.1 5.3 fusion.107
  664.4 10.3 %psum.14 = f32[256]{0:T(256)S(1)} all-reduce(f32[256]{0:T(256)S(1)} %get-tuple-element.55), channel_id=1, replica_groups=mesh['ep'=8,'tp'=4] {'tp'}, use_global_device_ids=true, to_apply=%region_24.25 | all-reduce | flops 256 | bytes 2048 | tf_op jit(solution)/shard_map/psum | solution.py:303
  677.4 3.6 all-to-all-start.1
  681.4 47.9 %psum.15 = f32[4352]{0:T(1024)S(1)} all-reduce(f32[4352]{0:T(1024)S(1)} %pad_maximum_fusion.10), channel_id=1, replica_groups=mesh['ep'=8,'tp'=4] {'ep','tp'}, use_global_device_ids=true, to_apply=%region_31.32 | all-reduce | flops 4352 | bytes 34816 | tf_op jit(solution)/shard_map/psum | solution.py:311
  732.4 4.0 reduce-scatter.17.cloned.1.call-done
  (302 shorter events, 85.5 us)
Async XLA Ops:
  7.2 341.5 %copy-start = (bf16[2,192,2048]{2,1,0:T(8,128)(2,1)S(1)}, bf16[2,192,2048]{2,1,0:T(8,128)(2,1)}, u32[]{:S(2)}) copy-start(bf16[2,192,2048]{2,1,0:T(8,128)(2,1)} %param.31) | copy-start | bytes 4718596
  8.7 18.4 %copy-start.38 = (bf16[256,1024]{1,0:T(8,128)(2,1)S(1)}, bf16[256,1024]{1,0:T(8,128)(2,1)}, u32[]{:S(2)}) copy-start(bf16[256,1024]{1,0:T(8,128)(2,1)} %param.25) | copy-start | bytes 1572868
  10.9 14.9 %all-to-all-start = ((bf16[8,32,1024]{2,1,0:T(8,128)(2,1)}), bf16[8,32,1024]{2,1,0:T(8,128)(2,1)S(1)}, u32[]{:S(2)}, u32[]{:S(2)}) async-start(bf16[8,32,1024]{2,1,0:T(8,128)(2,1)} %bitcast), calls=%async_computation | async-start | bytes 1048576 | tf_op jit(solution)/shard_map/all_to_all | solution.py:103
  16.1 41.9 %all-gather.10.cloned.1.call-start = ((), (), s32[]{:S(2)}) async-start(), calls=%async_computation.8 | async-start | bytes 1310720 | tf_op jit(solution)/shard_map/all_gather | solution.py:139
  27.1 88.1 %all-gather.12.cloned.1.call-start = ((), (), s32[]{:S(2)}) async-start(), calls=%async_computation.9 | async-start | bytes 10616832 | tf_op jit(solution)/shard_map/all_gather | solution.py:143
  29.3 116.0 %all-gather.16.cloned.1.call-start = ((), (), s32[]{:S(2)}) async-start(), calls=%async_computation.13 | async-start | bytes 1310720 | tf_op jit(solution)/shard_map/all_gather | solution.py:140
  55.1 66.6 %copy-start.58 = (f32[128]{0:T(128)}, f32[128]{0:T(128)S(1)}, u32[]{:S(2)}) copy-start(f32[128]{0:T(128)S(1)} %mul.459) | copy-start | bytes 1540
  55.1 66.6 %copy-start.60 = (f32[128]{0:T(128)}, f32[128]{0:T(128)S(1)}, u32[]{:S(2)}) copy-start(f32[128]{0:T(128)S(1)} %mul.473) | copy-start | bytes 1540
  55.8 67.9 %copy-start.62 = (f32[64]{0:T(128)}, f32[64]{0:T(128)S(1)}, u32[]{:S(2)}) copy-start(f32[64]{0:T(128)S(1)} %multiply_power_fusion) | copy-start | bytes 772
  56.0 67.7 %copy-start.51 = (f32[256]{0:T(256)}, f32[256]{0:T(256)S(1)}, u32[]{:S(2)}) copy-start(f32[256]{0:T(256)S(1)} %convert_bitcast_fusion.1) | copy-start | bytes 3076
  57.9 68.3 %copy-start.31 = (f32[256,64]{1,0:T(8,128)}, f32[256,64]{1,0:T(8,128)S(1)}, u32[]{:S(2)}) copy-start(f32[256,64]{1,0:T(8,128)S(1)} %get-tuple-element.94) | copy-start | bytes 196612
  57.9 169.5 %all-gather.22.cloned.1.call-start = ((), (), s32[]{:S(2)}) async-start(), calls=%async_computation.20 | async-start | bytes 5242880 | tf_op jit(solution)/shard_map/all_gather | solution.py:206
  58.0 59.4 %copy-start.3 = (bf16[256,2048]{1,0:T(8,128)(2,1)S(1)}, bf16[256,2048]{1,0:T(8,128)(2,1)}, u32[]{:S(2)}) copy-start(bf16[256,2048]{1,0:T(8,128)(2,1)} %all-gather.10.cloned.1.call-done) | copy-start | bytes 3145732
  59.6 61.4 %copy-start.49 = (f32[256]{0:T(256)}, f32[256]{0:T(256)S(1)}, u32[]{:S(2)}) copy-start(f32[256]{0:T(256)S(1)} %add_rsqrt_fusion.3) | copy-start | bytes 3076
  139.3 143.2 %all-gather.18.cloned.1.call-start = ((), (), s32[]{:S(2)}) async-start(), calls=%async_computation.14 | async-start | bytes 9437184 | tf_op jit(solution)/shard_map/all_gather | solution.py:162
  145.3 193.2 %all-gather.14.cloned.1.call-start = ((), (), s32[]{:S(2)}) async-start(), calls=%async_computation.10 | async-start | bytes 9437184 | tf_op jit(solution)/shard_map/all_gather | solution.py:211
  237.8 223.3 %reduce-scatter.11.cloned.1.call-start = ((), (), s32[]{:S(2)}) async-start(), calls=%async_computation.15 | async-start | bytes 9437184 | tf_op jit(solution)/shard_map/reduce_scatter | solution.py:228
  357.2 22.0 %copy-start.14 = (bf16[2048,384]{1,0:T(8,128)(2,1)}, bf16[2048,384]{1,0:T(8,128)(2,1)S(1)}, u32[]{:S(2)}) copy-start(bf16[2048,384]{1,0:T(8,128)(2,1)S(1)} %get-tuple-element.61) | copy-start | bytes 4718596
  357.2 22.0 %copy-start.12 = (bf16[2048,384]{1,0:T(8,128)(2,1)}, bf16[2048,384]{1,0:T(8,128)(2,1)S(1)}, u32[]{:S(2)}) copy-start(bf16[2048,384]{1,0:T(8,128)(2,1)S(1)} %get-tuple-element.62) | copy-start | bytes 4718596
  389.4 71.7 %copy-start.25 = (bf16[2048,384]{1,0:T(8,128)(2,1)S(1)}, bf16[2048,384]{1,0:T(8,128)(2,1)}, u32[]{:S(2)}) copy-start(bf16[2048,384]{1,0:T(8,128)(2,1)} %get-tuple-element.60) | copy-start | bytes 4718596
  389.4 101.3 %reduce-scatter.13.cloned.1.call-start = ((), (), s32[]{:S(2)}) async-start(), calls=%async_computation.16 | async-start | bytes 1310720 | tf_op jit(solution)/shard_map/reduce_scatter | solution.py:231
  461.1 103.1 %reduce-scatter.7.cloned.1.call-start = ((), (), s32[]{:S(2)}) async-start(), calls=%async_computation.11 | async-start | bytes 9437184 | tf_op jit(solution)/shard_map/reduce_scatter | solution.py:233
  469.3 22.7 %copy-start.19 = (bf16[2,8,128,128]{2,3,1,0:T(8,128)(2,1)S(1)}, bf16[2,8,128,128]{2,3,1,0:T(8,128)(2,1)}, u32[]{:S(2)}) copy-start(bf16[2,8,128,128]{2,3,1,0:T(8,128)(2,1)} %copy-done.18) | copy-start | bytes 1572868
  469.3 124.3 %copy-start.5 = (bf16[256,2048]{1,0:T(8,128)(2,1)S(1)}, bf16[256,2048]{1,0:T(8,128)(2,1)}, u32[]{:S(2)}) copy-start(bf16[256,2048]{1,0:T(8,128)(2,1)} %reduce_sum.208) | copy-start | bytes 3145732
  469.3 124.3 %all-gather.20.cloned.1.call-start = ((), (), s32[]{:S(2)}) async-start(), calls=%async_computation.17 | async-start | bytes 1310720 | tf_op jit(solution)/shard_map/all_gather | solution.py:241
  490.7 170.7 %reduce-scatter.9.cloned.1.call-start = ((), (), s32[]{:S(2)}) async-start(), calls=%async_computation.12 | async-start | bytes 1310720 | tf_op jit(solution)/shard_map/reduce_scatter | solution.py:234
  564.2 32.4 %copy-start.42 = (f32[1,2,8,128]{3,1,2,0:T(2,128)S(1)}, f32[1,2,8,128]{3,1,2,0:T(2,128)}, u32[]{:S(2)}) copy-start(f32[1,2,8,128]{3,1,2,0:T(2,128)} %copy.118) | copy-start | bytes 24580
  564.2 32.4 %copy-start.56 = (f32[256]{0:T(256)S(1)}, f32[256]{0:T(256)}, u32[]{:S(2)}) copy-start(f32[256]{0:T(256)} %copy-done.55) | copy-start | bytes 3076
  564.2 98.6 %reduce-scatter.15.cloned.1.call-start = ((), (), s32[]{:S(2)}) async-start(), calls=%async_computation.18 | async-start | bytes 1310720 | tf_op jit(solution)/shard_map/reduce_scatter | solution.py:286
  617.7 118.8 %reduce-scatter.17.cloned.1.call-start = ((), (), s32[]{:S(2)}) async-start(), calls=%async_computation.19 | async-start | bytes 10616832 | tf_op jit(solution)/shard_map/reduce_scatter | solution.py:297
  664.4 66.1 %copy-start.68 = (s32[256]{0:T(256)S(1)}, s32[256]{0:T(256)}, u32[]{:S(2)}) copy-start(s32[256]{0:T(256)} %copy-done.67) | copy-start | bytes 3076
  677.4 53.1 %all-to-all-start.1 = ((bf16[8,32,1024]{2,1,0:T(8,128)(2,1)}), bf16[8,32,1024]{2,1,0:T(8,128)(2,1)S(1)}, u32[]{:S(2)}, u32[]{:S(2)}) async-start(bf16[8,32,1024]{2,1,0:T(8,128)(2,1)} %bitcast.46), calls=%async_computation.6 | async-start | bytes 1048576 | tf_op jit(solution)/shard_map/all_to_all | solution.py:103
  (60 other events, 273.8 us)
Sparse Core Ops, SparseCore 0:
  27.2 27.3 all-gather.9
  57.0 58.0 all-gather.11
  117.3 27.9 all-gather.15
  147.3 80.1 all-gather.21
  229.2 53.2 all-gather.17
  284.2 54.2 all-gather.13
  389.6 71.4 reduce-scatter.10
  463.4 27.2 reduce-scatter.12
  494.2 69.9 reduce-scatter.6
  565.6 27.9 all-gather.19
  595.9 26.6 reduce-scatter.8
  625.4 25.7 reduce-scatter.14
  654.7 81.7 reduce-scatter.16
